TPU v7x, 32 devices: a whole 2x2x4 slice. The times are simulated.
32 devices in a mesh: wide: 8 (over z, x), narrow: 4 (over y, core).
Axes of the slice: x: 2, y: 2, z: 4, core: 2. Of those that a mesh axis runs over, the one named last changes fastest.
Arguments:
- tokens: bfloat16 [64, 512, 768], P(('wide', 'narrow')), may hold values from -6 to 6
- doc_lengths: int32 [64], P(('wide', 'narrow')), may hold values from 30 to 512
- qkv_weight: bfloat16 [768, 2304], replicated, may hold values from -0.21875 to 0.21875
- query_bias: bfloat16 [768], replicated, may hold values from -3 to 3
- value_bias: bfloat16 [768], replicated, may hold values from -3 to 3
- out_weight: bfloat16 [768, 768], replicated, may hold values from -0.625 to 0.625
- out_bias: bfloat16 [768], replicated, may hold values from -1.75 to 1.75
- first_gain: bfloat16 [768], replicated, may hold values from 0.5 to 1.5
- first_shift: bfloat16 [768], replicated, may hold values from -1.75 to 1.75
- up_weight: bfloat16 [768, 3072], replicated, may hold values from -0.21875 to 0.21875
- up_bias: bfloat16 [3072], replicated, may hold values from -3 to 3
- down_weight: bfloat16 [3072, 768], replicated, may hold values from -0.15625 to 0.15625
- down_bias: bfloat16 [768], replicated, may hold values from -1.75 to 1.75
- second_gain: bfloat16 [768], replicated, may hold values from 0.5 to 1.5
- second_shift: bfloat16 [768], replicated, may hold values from -1.75 to 1.75
- dir_weight: bfloat16 [1536, 8], replicated, may hold values from -0.375 to 0.375
- dir_bias: bfloat16 [8], replicated, may hold values from -1 to 1
- segment_rows: int32 [64, 128], P(('wide', 'narrow')), may hold values from 0 to 511, as said below
- segment_slots: int32 [32, 256], P(('wide', 'narrow')), may hold values from 0 to 255, each once within a row
- pair_rows: int32 [32, 256, 2], P(('wide', 'narrow')), may hold values from 0 to 255
- pair_labels: int32 [32, 256], P(('wide', 'narrow')), may hold values from 0 to 7
- out_cotangent: bfloat16 [64, 512, 768], P(('wide', 'narrow')), may hold values from -6 to 6
Outputs:
- encoded: bfloat16 [64, 512, 768], P(('wide', 'narrow'))
- grad_tokens: bfloat16 [64, 512, 768], P(('wide', 'narrow'))
- grad_qkv_weight: float32 [768, 2304], P('narrow', 'wide')
- grad_query_bias: float32 [768], replicated
- grad_value_bias: float32 [768], replicated
- grad_out_weight: float32 [768, 768], P('narrow', 'wide')
- grad_out_bias: float32 [768], replicated
- grad_first_gain: float32 [768], replicated
- grad_first_shift: float32 [768], replicated
- grad_up_weight: float32 [768, 3072], P('narrow', 'wide')
- grad_up_bias: float32 [3072], replicated
- grad_down_weight: float32 [3072, 768], P('narrow', 'wide')
- grad_down_bias: float32 [768], replicated
- grad_second_gain: float32 [768], replicated
- grad_second_shift: float32 [768], replicated
- grad_dir_weight: float32 [1536, 8], replicated
- grad_dir_bias: float32 [8], replicated
Inputs may be any that keep to these rules, and one draw needn't show every extreme that they name: `segment_rows`: each value is below the token count of its document. `segment_slots`: each device's row holds every slot once.
All inputs are finite; a program needn't handle non-finite values.
Results may differ from a plain program's by a relative error of at most 0.02.
Values may be sent and summed in bfloat16 or wider, within the bound.
A program may use at most 192 MiB of HBM per device.

v0:
```python
import jax
import jax.numpy as jnp
from jax import lax
from jax.sharding import PartitionSpec as P

HEADS = 12
HEAD_DIM = 64
EXACT = lax.Precision.HIGHEST
MASKED = -1e30
EPSILON = 1e-05


def norm_forward(values, gain, shift):
    center = jnp.mean(values, -1, keepdims=True)
    centered = values - center
    inverse = lax.rsqrt(jnp.mean(centered * centered, -1, keepdims=True) + EPSILON)
    normed = centered * inverse
    return (normed * gain + shift, normed, inverse)


def norm_backward(grad, normed, inverse, gain):
    scaled = grad * gain
    first_mean = jnp.mean(scaled, -1, keepdims=True)
    second_mean = jnp.mean(scaled * normed, -1, keepdims=True)
    return (
        (scaled - first_mean - normed * second_mean) * inverse,
        jnp.sum(grad * normed, 0),
        jnp.sum(grad, 0),
    )


def normal_cdf(values):
    return 0.5 * (1.0 + lax.erf(values * 0.7071067811865476))


def on_device(
    tokens,
    doc_lengths,
    qkv_weight,
    query_bias,
    value_bias,
    out_weight,
    out_bias,
    first_gain,
    first_shift,
    up_weight,
    up_bias,
    down_weight,
    down_bias,
    second_gain,
    second_shift,
    dir_weight,
    dir_bias,
    segment_rows,
    segment_slots,
    pair_rows,
    pair_labels,
    out_cotangent,
):
    doc_count, length, model_width = tokens.shape
    score_scale = HEAD_DIM ** (-0.5)
    token_rows = tokens.reshape(doc_count * length, model_width)
    allowed = lax.broadcasted_iota(jnp.int32, (doc_count, length), 1) < doc_lengths[:, None]
    allowed_rows = allowed.reshape(-1, 1).astype(jnp.float32)
    bias_row = jnp.concatenate([query_bias, jnp.zeros_like(query_bias), value_bias]).astype(
        jnp.float32
    )
    qkv = (jnp.dot(token_rows, qkv_weight, preferred_element_type=jnp.float32) + bias_row).astype(
        jnp.bfloat16
    )

    def split_heads(doc_block, which):
        return doc_block[:, which * model_width : (which + 1) * model_width].reshape(
            length, HEADS, HEAD_DIM
        )

    def scores_of(queries, key_rows, doc_mask):
        scores = (
            jnp.einsum("qhd,khd->hqk", queries, key_rows, preferred_element_type=jnp.float32)
            * score_scale
        )
        return jnp.where(doc_mask[None, None, :], scores, MASKED)

    mixed_parts = []
    log_totals = []
    for doc_index in range(doc_count):
        doc_block = qkv[doc_index * length : (doc_index + 1) * length]
        queries = split_heads(doc_block, 0)
        key_rows = split_heads(doc_block, 1)
        value_rows = split_heads(doc_block, 2)
        scores = scores_of(queries, key_rows, allowed[doc_index])
        highest = jnp.max(scores, -1, keepdims=True)
        powers = jnp.exp(scores - highest)
        summed = jnp.sum(powers, -1, keepdims=True)
        attention = (powers / summed).astype(jnp.bfloat16)
        log_totals.append(highest + jnp.log(summed))
        mixed_parts.append(
            jnp.einsum(
                "hqk,khd->qhd", attention, value_rows, preferred_element_type=jnp.float32
            ).reshape(length, model_width)
        )
    mixed = jnp.concatenate(mixed_parts).astype(jnp.bfloat16)
    attended = jnp.dot(mixed, out_weight, preferred_element_type=jnp.float32) + out_bias.astype(
        jnp.float32
    )
    resid_one = token_rows.astype(jnp.float32) + attended
    hidden_one, normed_one, inverse_one = norm_forward(
        resid_one, first_gain.astype(jnp.float32), first_shift.astype(jnp.float32)
    )
    hidden_low = hidden_one.astype(jnp.bfloat16)
    upper_pre = jnp.dot(hidden_low, up_weight, preferred_element_type=jnp.float32) + up_bias.astype(
        jnp.float32
    )
    cumulative = normal_cdf(upper_pre)
    active = (upper_pre * cumulative).astype(jnp.bfloat16)
    lowered = jnp.dot(active, down_weight, preferred_element_type=jnp.float32) + down_bias.astype(
        jnp.float32
    )
    resid_two = hidden_one + lowered
    second_float = second_gain.astype(jnp.float32)
    normed_out, normed_two, inverse_two = norm_forward(
        resid_two, second_float, second_shift.astype(jnp.float32)
    )
    encoded_rows = (normed_out * allowed_rows).astype(jnp.bfloat16)
    doc_starts = lax.broadcasted_iota(jnp.int32, (doc_count, 1), 0) * length
    picked_rows = (segment_rows + doc_starts).reshape(-1)
    picked = encoded_rows[picked_rows]
    slots = segment_slots.reshape(-1)
    outgoing = jnp.zeros_like(picked).at[slots].set(picked)
    arrived = lax.all_to_all(outgoing, "wide", split_axis=0, concat_axis=0, tiled=True)
    pairs = pair_rows.reshape(-1, 2)
    labels = pair_labels.reshape(-1)
    first_rows = arrived[pairs[:, 0]]
    second_rows = arrived[pairs[:, 1]]
    logits = (
        jnp.dot(first_rows, dir_weight[:model_width], preferred_element_type=jnp.float32)
        + jnp.dot(second_rows, dir_weight[model_width:], preferred_element_type=jnp.float32)
        + dir_bias.astype(jnp.float32)
    )
    powers_head = jnp.exp(logits - jnp.max(logits, -1, keepdims=True))
    chance = powers_head / jnp.sum(powers_head, -1, keepdims=True)
    classes = lax.broadcasted_iota(jnp.int32, logits.shape, 1)
    delta = chance - (labels[:, None] == classes).astype(jnp.float32)
    first_float = first_rows.astype(jnp.float32)
    second_rows_float = second_rows.astype(jnp.float32)
    grad_dir_weight = jnp.concatenate(
        [
            jnp.dot(first_float.T, delta, precision=EXACT, preferred_element_type=jnp.float32),
            jnp.dot(
                second_rows_float.T, delta, precision=EXACT, preferred_element_type=jnp.float32
            ),
        ]
    )
    grad_dir_bias = jnp.sum(delta, 0)
    dir_float = dir_weight.astype(jnp.float32)
    grad_first = jnp.dot(
        delta, dir_float[:model_width].T, precision=EXACT, preferred_element_type=jnp.float32
    )
    grad_second = jnp.dot(
        delta, dir_float[model_width:].T, precision=EXACT, preferred_element_type=jnp.float32
    )
    grad_arrived = jnp.zeros((arrived.shape[0], model_width), jnp.float32)
    grad_arrived = grad_arrived.at[pairs[:, 0]].add(grad_first).at[pairs[:, 1]].add(grad_second)
    returned = lax.all_to_all(
        grad_arrived.astype(jnp.bfloat16), "wide", split_axis=0, concat_axis=0, tiled=True
    )
    grad_picked = returned[slots].astype(jnp.float32)
    grad_encoded = (
        out_cotangent.reshape(-1, model_width).astype(jnp.float32).at[picked_rows].add(grad_picked)
    )
    grad_encoded = grad_encoded * allowed_rows
    grad_two, grad_second_gain, grad_second_shift = norm_backward(
        grad_encoded, normed_two, inverse_two, second_float
    )
    grad_lowered = grad_two.astype(jnp.bfloat16)
    grad_down_weight = jnp.einsum(
        "rf,rd->fd", active, grad_lowered, preferred_element_type=jnp.float32
    )
    grad_down_bias = jnp.sum(grad_lowered.astype(jnp.float32), 0)
    grad_active = jnp.einsum(
        "rd,fd->rf", grad_lowered, down_weight, preferred_element_type=jnp.float32
    )
    density = jnp.exp(-0.5 * upper_pre * upper_pre) * 0.3989422804014327
    grad_upper = (grad_active * (cumulative + upper_pre * density)).astype(jnp.bfloat16)
    grad_up_weight = jnp.einsum(
        "rd,rf->df", hidden_low, grad_upper, preferred_element_type=jnp.float32
    )
    grad_up_bias = jnp.sum(grad_upper.astype(jnp.float32), 0)
    grad_hidden = grad_two + jnp.einsum(
        "rf,df->rd", grad_upper, up_weight, preferred_element_type=jnp.float32
    )
    grad_one, grad_first_gain, grad_first_shift = norm_backward(
        grad_hidden, normed_one, inverse_one, first_gain.astype(jnp.float32)
    )
    grad_attended = grad_one.astype(jnp.bfloat16)
    grad_out_weight = jnp.einsum(
        "rd,re->de", mixed, grad_attended, preferred_element_type=jnp.float32
    )
    grad_out_bias = jnp.sum(grad_attended.astype(jnp.float32), 0)
    grad_mixed = jnp.einsum(
        "re,de->rd", grad_attended, out_weight, preferred_element_type=jnp.float32
    ).astype(jnp.bfloat16)
    grad_parts = []
    for doc_index in range(doc_count):
        doc_block = qkv[doc_index * length : (doc_index + 1) * length]
        queries = split_heads(doc_block, 0)
        key_rows = split_heads(doc_block, 1)
        value_rows = split_heads(doc_block, 2)
        scores = scores_of(queries, key_rows, allowed[doc_index])
        attention = jnp.exp(scores - log_totals[doc_index])
        grad_doc = grad_mixed[doc_index * length : (doc_index + 1) * length].reshape(
            length, HEADS, HEAD_DIM
        )
        grad_chance = jnp.einsum(
            "qhd,khd->hqk", grad_doc, value_rows, preferred_element_type=jnp.float32
        )
        inner = jnp.sum(grad_chance * attention, -1, keepdims=True)
        grad_scores = (attention * (grad_chance - inner)).astype(jnp.bfloat16)
        grad_query = (
            jnp.einsum("hqk,khd->qhd", grad_scores, key_rows, preferred_element_type=jnp.float32)
            * score_scale
        )
        grad_key = (
            jnp.einsum("hqk,qhd->khd", grad_scores, queries, preferred_element_type=jnp.float32)
            * score_scale
        )
        grad_value = jnp.einsum(
            "hqk,qhd->khd",
            attention.astype(jnp.bfloat16),
            grad_doc,
            preferred_element_type=jnp.float32,
        )
        grad_parts.append(
            jnp.concatenate(
                [
                    grad_query.reshape(length, model_width),
                    grad_key.reshape(length, model_width),
                    grad_value.reshape(length, model_width),
                ],
                axis=1,
            )
        )
    grad_qkv = jnp.concatenate(grad_parts).astype(jnp.bfloat16)
    grad_qkv_float = grad_qkv.astype(jnp.float32)
    grad_query_bias = jnp.sum(grad_qkv_float[:, :model_width], 0)
    grad_value_bias = jnp.sum(grad_qkv_float[:, 2 * model_width :], 0)
    grad_qkv_weight = jnp.einsum(
        "rd,re->de", token_rows, grad_qkv, preferred_element_type=jnp.float32
    )
    grad_tokens = (
        jnp.einsum("re,de->rd", grad_qkv, qkv_weight, preferred_element_type=jnp.float32) + grad_one
    ).astype(jnp.bfloat16)
    matrices = (grad_qkv_weight, grad_out_weight, grad_up_weight, grad_down_weight)
    partial_sums = (
        lax.psum_scatter(
            matrices[0].astype(jnp.bfloat16), "wide", scatter_dimension=1, tiled=True
        ).astype(jnp.float32),
        lax.psum_scatter(
            matrices[1].astype(jnp.bfloat16), "wide", scatter_dimension=1, tiled=True
        ).astype(jnp.float32),
        lax.psum_scatter(
            matrices[2].astype(jnp.bfloat16), "wide", scatter_dimension=1, tiled=True
        ).astype(jnp.float32),
        lax.psum_scatter(
            matrices[3].astype(jnp.bfloat16), "wide", scatter_dimension=1, tiled=True
        ).astype(jnp.float32),
    )
    summed_mats = (
        lax.psum_scatter(
            partial_sums[0].astype(jnp.bfloat16), "narrow", scatter_dimension=0, tiled=True
        ).astype(jnp.float32),
        lax.psum_scatter(
            partial_sums[1].astype(jnp.bfloat16), "narrow", scatter_dimension=0, tiled=True
        ).astype(jnp.float32),
        lax.psum_scatter(
            partial_sums[2].astype(jnp.bfloat16), "narrow", scatter_dimension=0, tiled=True
        ).astype(jnp.float32),
        lax.psum_scatter(
            partial_sums[3].astype(jnp.bfloat16), "narrow", scatter_dimension=0, tiled=True
        ).astype(jnp.float32),
    )
    smalls = lax.psum(
        (
            grad_query_bias,
            grad_value_bias,
            grad_out_bias,
            grad_first_gain,
            grad_first_shift,
            grad_up_bias,
            grad_down_bias,
            grad_second_gain,
            grad_second_shift,
            grad_dir_weight,
            grad_dir_bias,
        ),
        ("wide", "narrow"),
    )
    return (
        encoded_rows.reshape(tokens.shape),
        grad_tokens.reshape(tokens.shape),
        summed_mats[0],
        smalls[0],
        smalls[1],
        summed_mats[1],
        smalls[2],
        smalls[3],
        smalls[4],
        summed_mats[2],
        smalls[5],
        summed_mats[3],
        smalls[6],
        smalls[7],
        smalls[8],
        smalls[9],
        smalls[10],
    )


def solution(mesh):
    placed = (
        P(("wide", "narrow"), None, None),
        P(("wide", "narrow")),
        P(),
        P(),
        P(),
        P(),
        P(),
        P(),
        P(),
        P(),
        P(),
        P(),
        P(),
        P(),
        P(),
        P(),
        P(),
        P(("wide", "narrow"), None),
        P(("wide", "narrow"), None),
        P(("wide", "narrow"), None, None),
        P(("wide", "narrow"), None),
        P(("wide", "narrow"), None, None),
    )
    return jax.shard_map(
        on_device,
        mesh=mesh,
        in_specs=placed,
        out_specs=(
            P(("wide", "narrow"), None, None),
            P(("wide", "narrow"), None, None),
            P("narrow", "wide"),
            P(),
            P(),
            P("narrow", "wide"),
            P(),
            P(),
            P(),
            P("narrow", "wide"),
            P(),
            P("narrow", "wide"),
            P(),
            P(),
            P(),
            P(),
            P(),
        ),
        check_vma=False,
    )
```

profile of v0, /device:TPU:0, one launch (start us, length us, event | category | flops | bytes accessed | tf_op | source)
XLA Modules:
  0.0 747.2 jit_solution(5606578285930874321)
XLA Ops:
  20.7 5.9 add_convert_fusion
  26.6 2.3 fusion.56
  28.8 2.3 copy.79
  31.1 2.3 copy.83
  33.5 2.3 copy.82
  35.7 2.3 copy.81
  38.0 2.3 copy.78
  40.4 2.3 copy.77
  42.7 4.1 fusion.59
  48.7 2.6 copy-done.1
  51.5 2.6 fusion.27
  54.2 3.0 fusion.58
  57.3 1.9 fusion.7
  59.2 2.6 copy-done.2
  62.0 2.4 fusion.26
  66.9 13.4 %multiply_convert_fusion.2 = (bf16[1024,3072]{1,0:T(8,128)(2,1)S(1)}, f32[1024,3072]{1,0:T(8,128)}) fusion(f32[3072]{0:T(1024)S(1)} %copy-done.46, bf16[768,3072]{1,0:T(8,128)(2,1)} %param.31, f32[1024,768]{1,0:T(8,128)S(1)} %get-tuple-element.114, f32[768]{0:T(1024)S(1)} %copy-done.50, f32[768]{0:T(1024)S(1)} %convert_element_type.164, ...), kind=kOutput, calls=%fused_computation.22 | convolution fusion | flops 4854644736 | bytes 26765312 | tf_op jit(solution)/shard_map/dot_general | solution.py:111
  80.4 5.4 fusion.61
  89.3 4.9 scatter_custom_fusion
  94.2 7.7 %all-to-all-start = ((bf16[8,32,768]{2,1,0:T(8,128)(2,1)}), bf16[8,32,768]{2,1,0:T(8,128)(2,1)}, u32[]{:S(2)}, u32[]{:S(2)}) async-start(bf16[8,32,768]{2,1,0:T(8,128)(2,1)} %bitcast.144), calls=%async_computation | async-start | bytes 786432 | tf_op jit(solution)/shard_map/all_to_all | solution.py:130
  105.0 8.6 %all-to-all-done = bf16[8,32,768]{2,1,0:T(8,128)(2,1)} async-done(((bf16[8,32,768]{2,1,0:T(8,128)(2,1)}), bf16[8,32,768]{2,1,0:T(8,128)(2,1)}, u32[]{:S(2)}, u32[]{:S(2)}) %all-to-all-start) | async-done | bytes 393248 | tf_op jit(solution)/shard_map/all_to_all | solution.py:130
  113.6 3.3 gather_fusion.1
  117.0 3.2 gather_fusion
  124.0 2.1 fusion.36
  126.2 2.1 fusion.39
  128.3 3.7 scatter_custom_fusion.1
  132.0 4.8 scatter_fusion
  136.8 1.9 convert_element_type.179
  138.7 4.1 all-to-all-start.1
  146.9 3.3 bitcast_convert_fusion
  150.2 3.9 all-to-all-done.1
  154.0 8.2 %scatter_custom_fusion.3 = f32[1024,768]{1,0:T(8,128)} fusion(f32[1024,768]{1,0:T(8,128)} %bitcast_convert_fusion, s32[256]{0:T(256)} %bitcast.154, bf16[256,768]{1,0:T(8,128)(2,1)} %bitcast.24, s32[1024]{0:T(1024)} %pad_clamp_fusion), kind=kCustom, calls=%fused_computation.84 | custom fusion | flops 393216 | bytes 3543040 | tf_op jit(solution)/shard_map/scatter-add | solution.py:169
  162.3 5.0 multiply_reduce_fusion.2
  167.4 1.9 convert_reduce_fusion.1
  169.4 13.5 %convert_reduce_fusion = (f32[3072]{0:T(1024)}, bf16[1024,3072]{1,0:T(8,128)(2,1)S(1)}) fusion(f32[1024,3072]{1,0:T(8,128)} %get-tuple-element.116, f32[3072]{0:T(1024)S(1)} %copy-done.47, bf16[3072,768]{1,0:T(8,128)(2,1)S(1)} %bitcast.165, f32[1024,768]{1,0:T(8,128)S(1)} %get-tuple-element.94), kind=kOutput, calls=%fused_computation.15 | convolution fusion | flops 4873516032 | bytes 26763264 | tf_op jit(solution)/shard_map/rd,fd->rf/dot_general | solution.py:180
  182.9 6.5 multiply_reduce_fusion.3
  192.9 2.5 convolution_convert_fusion.4
  195.4 3.7 convolution_convert_fusion.3
  199.3 10.6 %multiply_reduce_fusion.1 = (f32[12,512]{1,0:T(8,128)S(1)}, f32[12,512,512]{1,2,0:T(8,128)}) fusion(f32[12,512,512]{1,2,0:T(8,128)} %copy-done.1, f32[12,512]{1,0:T(8,128)S(1)} %copy-done.28, bf16[512,12,64]{0,2,1:T(8,128)(2,1)S(1)} %bitcast.114, bf16[512,12,64]{0,2,1:T(8,128)(2,1)S(1)} %bitcast.131), kind=kOutput, calls=%fused_computation.20 | convolution fusion | flops 412084224 | bytes 26787840 | tf_op jit(solution)/shard_map/qhd,khd->hqk/dot_general | solution.py:214
  212.2 10.8 %multiply_convert_fusion.1 = bf16[12,512,512]{1,2,0:T(8,128)(2,1)} fusion(f32[12,512,512]{1,2,0:T(8,128)} %get-tuple-element.125, f32[12,512,512]{1,2,0:T(8,128)S(1)} %bitcast.104, f32[12,512]{1,0:T(8,128)S(1)} %get-tuple-element.124, f32[12,512]{1,0:T(8,128)S(1)} %copy-done.28), kind=kLoop, calls=%fused_computation.19 | loop fusion | flops 12582912 | bytes 31506432 | tf_op jit(solution)/shard_map/convert_element_type | solution.py:218
  223.0 5.9 multiply_convert_fusion.6
  228.9 4.8 multiply_convert_fusion.7
  233.7 3.0 fusion.23
  236.7 6.7 multiply_reduce_fusion
  243.4 10.7 %multiply_convert_fusion = bf16[12,512,512]{1,2,0:T(8,128)(2,1)S(1)} fusion(f32[12,512,512]{1,2,0:T(8,128)} %get-tuple-element.123, f32[12,512,512]{1,2,0:T(8,128)} %copy-done.2, f32[12,512]{1,0:T(8,128)} %get-tuple-element.122, f32[12,512]{1,0:T(8,128)} %log_add_fusion), kind=kLoop, calls=%fused_computation.16 | loop fusion | flops 12582912 | bytes 31506432 | tf_op jit(solution)/shard_map/convert_element_type | solution.py:218
  254.2 2.0 multiply_convert_fusion.4
  257.8 2.0 fusion.20
  260.8 29.7 %fusion.18 = bf16[768,2304]{0,1:T(8,128)(2,1)} fusion(bf16[1024,768]{1,0:T(8,128)(2,1)S(1)} %bitcast.170, bf16[512,768]{0,1:T(8,128)(2,1)S(1)} %bitcast.134, bf16[512,768]{0,1:T(8,128)(2,1)S(1)} %bitcast.141, bf16[512,768]{0,1:T(8,128)(2,1)S(1)} %bitcast.125, bf16[512,768]{0,1:T(8,128)(2,1)S(1)} %bitcast.135, bf16[512,768]{0,1:T(8,128)(2,1)S(1)} %bitcast.140, ...), kind=kOutput, calls=%fused_computation.45 | convolution fusion | flops 3653959680 | bytes 9830400 | tf_op jit(solution)/shard_map/rd,re->de/dot_general | solution.py:247
  290.6 10.7 %convolution_convert_fusion.1 = bf16[768,3072]{1,0:T(8,128)(2,1)} fusion(bf16[1024,3072]{1,0:T(8,128)(2,1)} %copy-done.63, f32[1024,768]{1,0:T(8,128)} %copy-done.6, f32[768]{0:T(1024)} %convert_element_type.165, f32[768]{0:T(1024)S(1)} %copy-done.42, f32[1024]{0:T(1024)} %copy-done.43, f32[1024]{0:T(1024)S(1)} %copy-done.40), kind=kOutput, calls=%fused_computation.42 | convolution fusion | flops 4838129664 | bytes 14170112 | tf_op jit(solution)/shard_map/rd,rf->df/dot_general | solution.py:185
  301.3 6.7 copy.105
  308.0 10.1 %convolution_convert_fusion = bf16[3072,768]{0,1:T(8,128)(2,1)} fusion(bf16[1024,3072]{1,0:T(8,128)(2,1)} %copy-done.64, f32[1024,768]{1,0:T(8,128)} %copy-done.22), kind=kOutput, calls=%fused_computation.41 | convolution fusion | flops 4834983936 | bytes 14155776 | tf_op jit(solution)/shard_map/rf,rd->fd/dot_general | solution.py:176
  320.0 68.3 %reduce-scatter.15.cloned.1.call-done = bf16[768,288]{0,1:T(8,128)(2,1)} async-done(((bf16[768,2304]{0,1:T(8,128)(2,1)}), bf16[768,288]{0,1:T(8,128)(2,1)}) %reduce-scatter.15.cloned.1.call-update) | async-done | bytes 442384 | tf_op jit(solution)/shard_map/reduce_scatter | solution.py:255
  388.3 2.1 copy.101
  390.5 96.5 %reduce-scatter.29.cloned.1.call-done = bf16[384,768]{1,0:T(8,128)(2,1)} async-done(((bf16[3072,768]{1,0:T(8,128)(2,1)}), bf16[384,768]{1,0:T(8,128)(2,1)}) %reduce-scatter.29.cloned.1.call-update) | async-done | bytes 589840
  487.0 2.1 copy.106
  489.1 1.9 fusion.64
  491.0 1.9 fusion.63
  492.9 92.7 %reduce-scatter.21.cloned.1.call-done = bf16[3072,96]{0,1:T(8,128)(2,1)} async-done(((bf16[3072,768]{0,1:T(8,128)(2,1)}), bf16[3072,96]{0,1:T(8,128)(2,1)}) %reduce-scatter.21.cloned.1.call-update) | async-done | bytes 589840 | tf_op jit(solution)/shard_map/reduce_scatter | solution.py:264
  587.3 7.3 fusion.54
  594.6 3.8 slice_reduce_fusion
  598.5 8.4 %add_convert_fusion.1 = bf16[1024,768]{1,0:T(8,128)(2,1)} fusion(f32[1024,768]{1,0:T(8,128)} %copy-done.25, bf16[768,2304]{1,0:T(8,128)(2,1)S(1)} %copy-done, bf16[512,768]{0,1:T(8,128)(2,1)} %bitcast.133, bf16[512,768]{0,1:T(8,128)(2,1)} %bitcast.143, bf16[512,768]{0,1:T(8,128)(2,1)} %bitcast.127, bf16[512,768]{0,1:T(8,128)(2,1)} %bitcast.137, ...), kind=kOutput, calls=%fused_computation.52 | convolution fusion | flops 3653763072 | bytes 12976128 | tf_op jit(solution)/shard_map/re,de->rd/dot_general | solution.py:251
  611.2 21.5 %reduce-scatter.25.cloned.1.call-done = bf16[192,288]{1,0:T(8,128)(2,1)} async-done(((bf16[768,288]{1,0:T(8,128)(2,1)}), bf16[192,288]{1,0:T(8,128)(2,1)}) %reduce-scatter.25.cloned.1.call-update) | async-done | bytes 110608
  636.1 21.3 %reduce-scatter.19.cloned.1.call-done = bf16[192,384]{1,0:T(8,128)(2,1)} async-done(((bf16[768,384]{1,0:T(8,128)(2,1)}), bf16[192,384]{1,0:T(8,128)(2,1)}) %reduce-scatter.19.cloned.1.call-update) | async-done | bytes 147472 | tf_op jit(solution)/shard_map/reduce_scatter | solution.py:275
  659.0 23.2 %reduce-scatter.23.cloned.1.call-done = bf16[768,96]{0,1:T(8,128)(2,1)} async-done(((bf16[3072,96]{0,1:T(8,128)(2,1)}), bf16[768,96]{0,1:T(8,128)(2,1)}) %reduce-scatter.23.cloned.1.call-update) | async-done | bytes 147472 | tf_op jit(solution)/shard_map/reduce_scatter | solution.py:278
  683.8 41.7 %all-reduce.3.cloned.1.call-done = (f32[768]{0:T(1024)}, f32[768]{0:T(1024)}, f32[768]{0:T(1024)}, f32[768]{0:T(1024)}, f32[768]{0:T(1024)}, /*index=5*/f32[3072...) async-done(((f32[768]{0:T(1024)}, f32[768]{0:T(1024)}, f32[768]{0:T(1024)}, f32[768]{0:T(1024)}, f32[768]{0:T(1024)}, ...) | async-done | bytes 86064 | tf_op jit(solution)/shard_map/psum | solution.py:282
  (246 shorter events, 69.1 us)
Async XLA Ops:
  8.0 12.7 %copy-start = (bf16[768,2304]{1,0:T(8,128)(2,1)S(1)}, bf16[768,2304]{1,0:T(8,128)(2,1)}, u32[]{:S(2)}) copy-start(bf16[768,2304]{1,0:T(8,128)(2,1)} %param.24) | copy-start | bytes 10616836
  9.0 7.2 copy-start.49
  11.0 69.3 %copy-start.41 = (f32[768]{0:T(1024)}, f32[768]{0:T(1024)S(1)}, u32[]{:S(2)}) copy-start(f32[768]{0:T(1024)S(1)} %convert_element_type.164) | copy-start | bytes 9220
  18.1 68.2 %copy-start.35 = (f32[1,4,2,128]{3,1,2,0:T(4,128)}, f32[1,4,2,128]{3,1,2,0:T(4,128)S(1)}, u32[]{:S(2)}) copy-start(f32[1,4,2,128]{3,1,2,0:T(4,128)S(1)} %copy.107) | copy-start | bytes 12292
  28.8 13.9 %copy-start.55 = (pred[512]{0:T(512)(128)(4,1)S(1)}, pred[512]{0:T(512)(128)(4,1)}, u32[]{:S(2)}) copy-start(pred[512]{0:T(512)(128)(4,1)} %get-tuple-element.78) | copy-start | bytes 1540
  46.8 4.5 copy-start.1
  46.8 4.7 copy-start.31
  46.8 4.7 copy-start.20
  48.7 5.5 copy-start.33
  54.2 10.3 %copy-start.59 = (bf16[12,64,512]{2,1,0:T(8,128)(2,1)}, bf16[12,64,512]{2,1,0:T(8,128)(2,1)S(1)}, u32[]{:S(2)}) copy-start(bf16[12,64,512]{2,1,0:T(8,128)(2,1)S(1)} %fusion.27) | copy-start | bytes 2359300
  57.3 4.5 copy-start.2
  57.3 4.7 copy-start.32
  57.3 4.7 copy-start.18
  59.2 5.3 copy-start.34
  66.2 14.0 %copy-start.6 = (f32[1024,768]{1,0:T(8,128)}, f32[1024,768]{1,0:T(8,128)S(1)}, u32[]{:S(2)}) copy-start(f32[1024,768]{1,0:T(8,128)S(1)} %get-tuple-element.114) | copy-start | bytes 9437188
  66.3 14.0 %copy-start.39 = (f32[1024]{0:T(1024)}, f32[1024]{0:T(1024)S(1)}, u32[]{:S(2)}) copy-start(f32[1024]{0:T(1024)S(1)} %broadcast_multiply_fusion.5) | copy-start | bytes 12292
  66.3 14.0 %slice-start.9 = ((s8[4718592]{0:T(1024)(128)(4,1)}), s8[4194304]{0:T(1024)(128)(4,1)S(1)}, s32[]{:S(2)}) async-start(s8[4718592]{0:T(1024)(128)(4,1)} %bitcast.162), calls=%async_computation.28 | async-start | bytes 8388608
  66.8 13.5 %copy-start.43 = (f32[1024]{0:T(1024)}, f32[1024]{0:T(1024)S(1)}, u32[]{:S(2)}) copy-start(f32[1024]{0:T(1024)S(1)} %add_rsqrt_fusion.1) | copy-start | bytes 12292
  66.9 13.5 %copy-start.51 = (f32[768]{0:T(1024)S(1)}, f32[768]{0:T(1024)}, u32[]{:S(2)}) copy-start(f32[768]{0:T(1024)} %convert_element_type.169) | copy-start | bytes 9220
  66.9 13.5 %slice-start.10 = ((s8[4718592]{0:T(1024)(128)(4,1)}), s8[524288]{0:T(1024)(128)(4,1)S(1)}, s32[]{:S(2)}) async-start(s8[4718592]{0:T(1024)(128)(4,1)} %bitcast.162), calls=%async_computation.29 | async-start | bytes 1048576
  80.3 5.5 copy-start.64
  80.3 7.2 copy-start.45
  86.4 30.6 %copy-start.37 = (f32[1024]{0:T(1024)}, f32[1024]{0:T(1024)S(1)}, u32[]{:S(2)}) copy-start(f32[1024]{0:T(1024)S(1)} %add_rsqrt_fusion) | copy-start | bytes 12292
  94.2 19.4 %all-to-all-start = ((bf16[8,32,768]{2,1,0:T(8,128)(2,1)}), bf16[8,32,768]{2,1,0:T(8,128)(2,1)}, u32[]{:S(2)}, u32[]{:S(2)}) async-start(bf16[8,32,768]{2,1,0:T(8,128)(2,1)} %bitcast.144), calls=%async_computation | async-start | bytes 786432 | tf_op jit(solution)/shard_map/all_to_all | solution.py:130
  138.7 15.3 %all-to-all-start.1 = ((bf16[8,32,768]{2,1,0:T(8,128)(2,1)}), bf16[8,32,768]{2,1,0:T(8,128)(2,1)}, u32[]{:S(2)}, u32[]{:S(2)}) async-start(bf16[8,32,768]{2,1,0:T(8,128)(2,1)} %bitcast.145), calls=%async_computation.1 | async-start | bytes 786432 | tf_op jit(solution)/shard_map/all_to_all | solution.py:164
  142.8 175.4 %reduce-scatter.17.cloned.1.call-start = ((), (), s32[]{:S(2)}) async-start(), calls=%async_computation.11 | async-start | bytes 1327104 | tf_op jit(solution)/shard_map/reduce_scatter | solution.py:258
  162.3 5.1 copy-start.4
  162.3 5.1 copy-start.5
  162.3 5.1 copy-start.36
  162.3 5.1 copy-start.38
  162.3 7.0 slice-start.11
  167.4 15.4 %slice-start.13 = ((s8[4718592]{0:T(1024)(128)(4,1)}), s8[4194304]{0:T(1024)(128)(4,1)S(1)}, s32[]{:S(2)}) async-start(s8[4718592]{0:T(1024)(128)(4,1)} %bitcast.166), calls=%async_computation.32 | async-start | bytes 8388608
  169.3 13.5 %copy-start.22 = (f32[1024,768]{1,0:T(8,128)}, f32[1024,768]{1,0:T(8,128)S(1)}, u32[]{:S(2)}) copy-start(f32[1024,768]{1,0:T(8,128)S(1)} %get-tuple-element.94) | copy-start | bytes 9437188
  169.3 13.5 %copy-start.7 = (f32[1024,768]{1,0:T(8,128)S(1)}, f32[1024,768]{1,0:T(8,128)}, u32[]{:S(2)}) copy-start(f32[1024,768]{1,0:T(8,128)} %copy-done.6) | copy-start | bytes 9437188
  169.3 13.5 %copy-start.40 = (f32[1024]{0:T(1024)S(1)}, f32[1024]{0:T(1024)}, u32[]{:S(2)}) copy-start(f32[1024]{0:T(1024)} %copy-done.39) | copy-start | bytes 12292
  169.3 13.5 %copy-start.42 = (f32[768]{0:T(1024)S(1)}, f32[768]{0:T(1024)}, u32[]{:S(2)}) copy-start(f32[768]{0:T(1024)} %copy-done.41) | copy-start | bytes 9220
  169.3 13.5 %copy-start.44 = (f32[1024]{0:T(1024)S(1)}, f32[1024]{0:T(1024)}, u32[]{:S(2)}) copy-start(f32[1024]{0:T(1024)} %copy-done.43) | copy-start | bytes 12292
  169.4 13.5 %slice-start.14 = ((s8[4718592]{0:T(1024)(128)(4,1)}), s8[524288]{0:T(1024)(128)(4,1)S(1)}, s32[]{:S(2)}) async-start(s8[4718592]{0:T(1024)(128)(4,1)} %bitcast.166), calls=%async_computation.33 | async-start | bytes 1048576
  182.8 6.6 copy-start.63
  189.4 3.5 copy-start.60
  195.4 3.9 copy-start.21
  195.4 3.9 copy-start.28
  199.3 10.7 %copy-start.11 = (bf16[512,768]{0,1:T(8,128)(2,1)}, bf16[512,768]{0,1:T(8,128)(2,1)S(1)}, u32[]{:S(2)}) copy-start(bf16[512,768]{0,1:T(8,128)(2,1)S(1)} %get-tuple-element.103) | copy-start | bytes 2359300
  199.3 10.7 %slice-start = ((s8[12582912]{0:T(1024)(128)(4,1)}), s8[4194304]{0:T(1024)(128)(4,1)S(1)}, s32[]{:S(2)}) async-start(s8[12582912]{0:T(1024)(128)(4,1)} %bitcast.103), calls=%async_computation.19 | async-start | bytes 8388608
  199.3 11.7 %slice-start.1 = ((s8[12582912]{0:T(1024)(128)(4,1)}), s8[4194304]{0:T(1024)(128)(4,1)S(1)}, s32[]{:S(2)}) async-start(s8[12582912]{0:T(1024)(128)(4,1)} %bitcast.103), calls=%async_computation.20 | async-start | bytes 8388608
  199.3 12.9 %slice-start.2 = ((s8[12582912]{0:T(1024)(128)(4,1)}), s8[4194304]{0:T(1024)(128)(4,1)S(1)}, s32[]{:S(2)}) async-start(s8[12582912]{0:T(1024)(128)(4,1)} %bitcast.103), calls=%async_computation.21 | async-start | bytes 8388608
  212.2 10.8 %copy-start.15 = (bf16[512,768]{0,1:T(8,128)(2,1)S(1)}, bf16[512,768]{0,1:T(8,128)(2,1)}, u32[]{:S(2)}) copy-start(bf16[512,768]{0,1:T(8,128)(2,1)} %copy.78) | copy-start | bytes 2359300
  212.2 21.5 %slice-start.6 = ((s8[12582912]{0:T(1024)(128)(4,1)}), s8[4194304]{0:T(1024)(128)(4,1)S(1)}, s32[]{:S(2)}) async-start(s8[12582912]{0:T(1024)(128)(4,1)} %bitcast.107), calls=%async_computation.25 | async-start | bytes 8388608
  212.2 21.5 %slice-start.7 = ((s8[12582912]{0:T(1024)(128)(4,1)}), s8[4194304]{0:T(1024)(128)(4,1)S(1)}, s32[]{:S(2)}) async-start(s8[12582912]{0:T(1024)(128)(4,1)} %bitcast.107), calls=%async_computation.26 | async-start | bytes 8388608
  223.0 5.9 copy-start.10
  223.0 10.7 %slice-start.8 = ((s8[12582912]{0:T(1024)(128)(4,1)}), s8[4194304]{0:T(1024)(128)(4,1)S(1)}, s32[]{:S(2)}) async-start(s8[12582912]{0:T(1024)(128)(4,1)} %bitcast.107), calls=%async_computation.27 | async-start | bytes 8388608
  228.9 4.8 copy-start.30
  243.4 145.0 %reduce-scatter.15.cloned.1.call-start = ((), (), s32[]{:S(2)}) async-start(), calls=%async_computation.10 | async-start | bytes 3981312 | tf_op jit(solution)/shard_map/reduce_scatter | solution.py:255
  243.4 10.8 %copy-start.14 = (bf16[512,768]{0,1:T(8,128)(2,1)S(1)}, bf16[512,768]{0,1:T(8,128)(2,1)}, u32[]{:S(2)}) copy-start(bf16[512,768]{0,1:T(8,128)(2,1)} %copy.82) | copy-start | bytes 2359300
  243.4 14.0 %slice-start.3 = ((s8[12582912]{0:T(1024)(128)(4,1)}), s8[4194304]{0:T(1024)(128)(4,1)S(1)}, s32[]{:S(2)}) async-start(s8[12582912]{0:T(1024)(128)(4,1)} %bitcast.105), calls=%async_computation.22 | async-start | bytes 8388608
  243.4 14.0 %slice-start.4 = ((s8[12582912]{0:T(1024)(128)(4,1)}), s8[4194304]{0:T(1024)(128)(4,1)S(1)}, s32[]{:S(2)}) async-start(s8[12582912]{0:T(1024)(128)(4,1)} %bitcast.105), calls=%async_computation.23 | async-start | bytes 8388608
  256.2 3.6 copy-start.27
  290.6 196.4 %reduce-scatter.29.cloned.1.call-start = ((), (), s32[]{:S(2)}) async-start(), calls=%async_computation.17 | async-start | bytes 5308416
  308.0 277.7 %reduce-scatter.21.cloned.1.call-start = ((), (), s32[]{:S(2)}) async-start(), calls=%async_computation.13 | async-start | bytes 5308416 | tf_op jit(solution)/shard_map/reduce_scatter | solution.py:264
  318.1 290.0 %reduce-scatter.27.cloned.1.call-start = ((), (), s32[]{:S(2)}) async-start(), calls=%async_computation.16 | async-start | bytes 245760
  320.0 312.7 %reduce-scatter.25.cloned.1.call-start = ((), (), s32[]{:S(2)}) async-start(), calls=%async_computation.15 | async-start | bytes 737280
  390.4 267.0 %reduce-scatter.19.cloned.1.call-start = ((), (), s32[]{:S(2)}) async-start(), calls=%async_computation.12 | async-start | bytes 737280 | tf_op jit(solution)/shard_map/reduce_scatter | solution.py:275
  489.1 193.1 %reduce-scatter.23.cloned.1.call-start = ((), (), s32[]{:S(2)}) async-start(), calls=%async_computation.14 | async-start | bytes 737280 | tf_op jit(solution)/shard_map/reduce_scatter | solution.py:278
  585.7 139.9 %all-reduce.3.cloned.1.call-start = ((), (), s32[]{:S(2)}) async-start(), calls=%async_computation.18 | async-start | bytes 189440 | tf_op jit(solution)/shard_map/psum | solution.py:282
  (27 other events, 60.0 us)
Sparse Core Ops, SparseCore 0:
  243.5 63.0 reduce-scatter.16
  310.2 78.0 reduce-scatter.14
  392.0 94.9 reduce-scatter.28
  490.5 95.1 reduce-scatter.20
  588.5 19.5 reduce-scatter.26
  610.5 22.1 reduce-scatter.24
  635.3 22.0 reduce-scatter.18
  660.1 22.0 reduce-scatter.22
Sparse Core Ops, SparseCore 1:
  598.5 126.9 all-reduce.2
where the time goes:
time: 756 us; the launch traced here: 747 us
  waiting for transfers between devices  379 us (50%)
  matrix products  170 us (22%)
  other arithmetic  94.5 us (12%)
  local copies, waits for them, and re-layouts  74.2 us (10%)
  between operations  16.8 us (2%)
  starting transfers between devices  12.4 us (2%)
    unnamed x12, waiting for transfers between devices  119 us
    reduce_scatter x1, waiting for transfers between devices, on_device(): lax.psum_scatter(matrices[3].astype(jnp.bfloat16), 'wide', scatter_dimens...  92.7 us
    reduce_scatter x1, waiting for transfers between devices, on_device(): lax.psum_scatter(matrices[0].astype(jnp.bfloat16), 'wide', scatter_dimens...  68.3 us
    unnamed x180, local copies, waits for them, and re-layouts  46 us
    psum x1, waiting for transfers between devices, on_device(): lax.psum((grad_query_bias, grad_value_bias, grad_out_bias, grad_first_gai...  41.7 us
    dot_general x1, matrix products, on_device(): jnp.einsum('rd,re->de', token_rows, grad_qkv, preferred_element_type=jnp....  29.7 us
    reduce_scatter x1, waiting for transfers between devices, on_device(): lax.psum_scatter(partial_sums[3].astype(jnp.bfloat16), 'narrow', scatter_...  23.2 us
    convert_element_type x2, other arithmetic, on_device(): grad_scores = (attention * (grad_chance - inner)).astype(jnp.bfloat16)  21.5 us
  transfers between devices with their start and end apart: 11, of which 10 were waited for; matrix products, arithmetic and copies ran while one was open for 16% of the time, Pallas kernels for 0%

commit v1 on v0

--- a/solution.py
+++ b/solution.py
@@ -8,6 +8,17 @@
 EXACT = lax.Precision.HIGHEST
 MASKED = -1e30
 EPSILON = 1e-05
+
+
+def in_blocks(shard, dim, size):
+    before, after = (shard.shape[:dim], shard.shape[dim + 1 :])
+    return jnp.moveaxis(shard.reshape(*before, size, -1, *after), dim, 0)
+
+
+def joined_along(blocks, dim):
+    blocks = jnp.moveaxis(blocks, 0, dim)
+    dims = blocks.shape
+    return blocks.reshape(*dims[:dim], dims[dim] * dims[dim + 1], *dims[dim + 2 :])
 
 
 def norm_forward(values, gain, shift):
@@ -127,7 +138,14 @@
     picked = encoded_rows[picked_rows]
     slots = segment_slots.reshape(-1)
     outgoing = jnp.zeros_like(picked).at[slots].set(picked)
-    arrived = lax.all_to_all(outgoing, "wide", split_axis=0, concat_axis=0, tiled=True)
+    size, mine = (lax.axis_size("wide"), lax.axis_index("wide"))
+    blocks = in_blocks(outgoing, 0, size)
+    outs = [blocks[mine]]
+    for step in range(1, size):
+        sent = blocks[mine ^ step]
+        outs.append(lax.ppermute(sent, "wide", [(i, i ^ step) for i in range(size)]))
+    blocks = jnp.stack(outs)[mine ^ jnp.arange(size)]
+    arrived = joined_along(blocks, 0)
     pairs = pair_rows.reshape(-1, 2)
     labels = pair_labels.reshape(-1)
     first_rows = arrived[pairs[:, 0]]

time: 756 us -> 769 us (1.017)
  local copies, waits for them, and re-layouts: 74.2 us -> 82.6 us
    ppermute x0 -> x7, starting transfers between devices: none -> 12.9 us  [on_device(): lax.ppermute(sent, 'wide', [(i, i ^ step) for i in range(size)])]
    all_to_all x1 -> x0, waiting for transfers between devices: 8.62 us -> none  [on_device(): lax.all_to_all(outgoing, 'wide', split_axis=0, concat_axis=0, tiled=True)]
    all_to_all x1 -> x0, starting transfers between devices: 7.7 us -> none  [on_device(): lax.all_to_all(outgoing, 'wide', split_axis=0, concat_axis=0, tiled=True)]
  transfers between devices with their start and end apart: 11 -> 17, of which waited for: 10 -> 11; matrix products, arithmetic and copies ran while one was open for 16% -> 17% of each run, Pallas kernels for 0% -> 0%
where the time goes in v1:
time: 769 us; the launch traced here: 760 us
  waiting for transfers between devices  374 us (49%)
  matrix products  170 us (22%)
  other arithmetic  97.7 us (13%)
  local copies, waits for them, and re-layouts  82.6 us (11%)
  starting transfers between devices  18.5 us (2%)
  between operations  16.9 us (2%)
    unnamed x12, waiting for transfers between devices  119 us
    reduce_scatter x1, waiting for transfers between devices, on_device(): lax.psum_scatter(matrices[3].astype(jnp.bfloat16), 'wide', scatter_dimens...  92.5 us
    reduce_scatter x1, waiting for transfers between devices, on_device(): lax.psum_scatter(matrices[0].astype(jnp.bfloat16), 'wide', scatter_dimens...  69.1 us
    unnamed x180, local copies, waits for them, and re-layouts  49.7 us
    psum x1, waiting for transfers between devices, on_device(): lax.psum((grad_query_bias, grad_value_bias, grad_out_bias, grad_first_gai...  41.6 us
    dot_general x1, matrix products, on_device(): jnp.einsum('rd,re->de', token_rows, grad_qkv, preferred_element_type=jnp....  29.7 us
    reduce_scatter x1, waiting for transfers between devices, on_device(): lax.psum_scatter(partial_sums[3].astype(jnp.bfloat16), 'narrow', scatter_...  23.2 us
    convert_element_type x2, other arithmetic, on_device(): grad_scores = (attention * (grad_chance - inner)).astype(jnp.bfloat16)  21.5 us
  transfers between devices with their start and end apart: 17, of which 11 were waited for; matrix products, arithmetic and copies ran while one was open for 17% of the time, Pallas kernels for 0%

profile of v1, /device:TPU:0, one launch (start us, length us, event | category | flops | bytes accessed | tf_op | source)
XLA Modules:
  0.0 760.3 jit_solution(12080092621451816105)
XLA Ops:
  19.5 5.9 add_convert_fusion
  25.3 2.3 fusion.57
  27.6 2.3 copy.79
  29.9 2.3 copy.83
  32.2 2.3 copy.82
  34.5 2.3 copy.81
  36.8 2.3 copy.78
  39.1 2.3 copy.77
  41.5 4.1 fusion.60
  47.5 2.6 copy-done.1
  50.3 2.6 fusion.27
  53.0 3.0 fusion.59
  58.0 2.6 copy-done.2
  60.8 2.4 fusion.26
  65.7 13.4 %multiply_convert_fusion.2 = (bf16[1024,3072]{1,0:T(8,128)(2,1)S(1)}, f32[1024,3072]{1,0:T(8,128)}) fusion(f32[3072]{0:T(1024)S(1)} %copy-done.45, bf16[768,3072]{1,0:T(8,128)(2,1)} %param.31, f32[1024,768]{1,0:T(8,128)S(1)} %get-tuple-element.122, f32[768]{0:T(1024)S(1)} %copy-done.48, f32[768]{0:T(1024)S(1)} %convert_element_type.164, ...), kind=kOutput, calls=%fused_computation.23 | convolution fusion | flops 4854644736 | bytes 26765312 | tf_op jit(solution)/shard_map/dot_general | solution.py:122
  79.1 5.4 fusion.62
  88.3 3.2 multiply_convert_fusion.3
  91.5 4.9 scatter_custom_fusion
  98.0 6.0 collective-permute-start.6
  105.0 1.9 collective-permute-start.3
  114.2 2.4 collective-permute-done.1
  118.3 3.3 collective-permute-done.2
  124.7 2.4 gather_fusion
  127.1 3.3 gather_fusion.2
  130.5 3.2 gather_fusion.1
  137.5 2.1 fusion.36
  139.7 2.1 fusion.39
  141.8 4.1 scatter_custom_fusion.1
  145.9 4.8 scatter_fusion
  150.7 1.9 convert_element_type.179
  152.6 5.0 all-to-all-start
  161.7 3.3 bitcast_convert_fusion
  165.0 1.9 all-to-all-done
  166.9 8.2 %scatter_custom_fusion.3 = f32[1024,768]{1,0:T(8,128)} fusion(f32[1024,768]{1,0:T(8,128)} %bitcast_convert_fusion, s32[256]{0:T(256)} %bitcast.186, bf16[256,768]{1,0:T(8,128)(2,1)} %bitcast.39, s32[1024]{0:T(1024)} %pad_clamp_fusion), kind=kCustom, calls=%fused_computation.85 | custom fusion | flops 393216 | bytes 3543040 | tf_op jit(solution)/shard_map/scatter-add | solution.py:187
  175.1 5.0 multiply_reduce_fusion.2
  182.2 13.4 %convert_reduce_fusion = (f32[3072]{0:T(1024)}, bf16[1024,3072]{1,0:T(8,128)(2,1)S(1)}) fusion(f32[1024,3072]{1,0:T(8,128)} %get-tuple-element.124, f32[3072]{0:T(1024)S(1)} %copy-done.46, bf16[3072,768]{1,0:T(8,128)(2,1)S(1)} %bitcast.197, f32[1024,768]{1,0:T(8,128)S(1)} %get-tuple-element.94), kind=kOutput, calls=%fused_computation.16 | convolution fusion | flops 4873516032 | bytes 26763264 | tf_op jit(solution)/shard_map/rd,fd->rf/dot_general | solution.py:198
  195.7 6.5 multiply_reduce_fusion.3
  205.7 2.5 convolution_convert_fusion.4
  208.2 3.7 convolution_convert_fusion.3
  212.1 10.6 %multiply_reduce_fusion.1 = (f32[12,512]{1,0:T(8,128)S(1)}, f32[12,512,512]{1,2,0:T(8,128)}) fusion(f32[12,512,512]{1,2,0:T(8,128)} %copy-done.1, f32[12,512]{1,0:T(8,128)S(1)} %copy-done.28, bf16[512,12,64]{0,2,1:T(8,128)(2,1)S(1)} %bitcast.146, bf16[512,12,64]{0,2,1:T(8,128)(2,1)S(1)} %bitcast.163), kind=kOutput, calls=%fused_computation.21 | convolution fusion | flops 412084224 | bytes 26787840 | tf_op jit(solution)/shard_map/qhd,khd->hqk/dot_general | solution.py:232
  225.0 10.8 %multiply_convert_fusion.1 = bf16[12,512,512]{1,2,0:T(8,128)(2,1)} fusion(f32[12,512,512]{1,2,0:T(8,128)} %get-tuple-element.133, f32[12,512,512]{1,2,0:T(8,128)S(1)} %bitcast.134, f32[12,512]{1,0:T(8,128)S(1)} %get-tuple-element.132, f32[12,512]{1,0:T(8,128)S(1)} %copy-done.28), kind=kLoop, calls=%fused_computation.20 | loop fusion | flops 12582912 | bytes 31506432 | tf_op jit(solution)/shard_map/convert_element_type | solution.py:236
  235.8 5.8 multiply_convert_fusion.6
  241.6 4.8 multiply_convert_fusion.7
  246.5 3.0 fusion.23
  249.5 6.7 multiply_reduce_fusion
  256.2 10.7 %multiply_convert_fusion = bf16[12,512,512]{1,2,0:T(8,128)(2,1)S(1)} fusion(f32[12,512,512]{1,2,0:T(8,128)} %get-tuple-element.131, f32[12,512,512]{1,2,0:T(8,128)} %copy-done.2, f32[12,512]{1,0:T(8,128)} %get-tuple-element.130, f32[12,512]{1,0:T(8,128)} %log_add_fusion), kind=kLoop, calls=%fused_computation.17 | loop fusion | flops 12582912 | bytes 31506432 | tf_op jit(solution)/shard_map/convert_element_type | solution.py:236
  267.0 2.0 multiply_convert_fusion.4
  270.6 2.0 fusion.20
  273.6 29.7 %fusion.18 = bf16[768,2304]{0,1:T(8,128)(2,1)} fusion(bf16[1024,768]{1,0:T(8,128)(2,1)S(1)} %bitcast.202, bf16[512,768]{0,1:T(8,128)(2,1)S(1)} %bitcast.166, bf16[512,768]{0,1:T(8,128)(2,1)S(1)} %bitcast.173, bf16[512,768]{0,1:T(8,128)(2,1)S(1)} %bitcast.157, bf16[512,768]{0,1:T(8,128)(2,1)S(1)} %bitcast.167, bf16[512,768]{0,1:T(8,128)(2,1)S(1)} %bitcast.172, ...), kind=kOutput, calls=%fused_computation.46 | convolution fusion | flops 3653959680 | bytes 9830400 | tf_op jit(solution)/shard_map/rd,re->de/dot_general | solution.py:265
  303.4 10.6 %convolution_convert_fusion.1 = bf16[768,3072]{1,0:T(8,128)(2,1)} fusion(bf16[1024,3072]{1,0:T(8,128)(2,1)} %copy-done.60, f32[1024,768]{1,0:T(8,128)} %copy-done.6, f32[768]{0:T(1024)} %convert_element_type.165, f32[768]{0:T(1024)S(1)} %copy-done.42, f32[1024]{0:T(1024)} %copy-done.43, f32[1024]{0:T(1024)S(1)} %copy-done.40), kind=kOutput, calls=%fused_computation.43 | convolution fusion | flops 4838129664 | bytes 14170112 | tf_op jit(solution)/shard_map/rd,rf->df/dot_general | solution.py:203
  314.0 6.7 copy.105
  320.7 10.1 %convolution_convert_fusion = bf16[3072,768]{0,1:T(8,128)(2,1)} fusion(bf16[1024,3072]{1,0:T(8,128)(2,1)} %copy-done.61, f32[1024,768]{1,0:T(8,128)} %copy-done.22), kind=kOutput, calls=%fused_computation.42 | convolution fusion | flops 4834983936 | bytes 14155776 | tf_op jit(solution)/shard_map/rf,rd->fd/dot_general | solution.py:194
  332.7 69.1 %reduce-scatter.15.cloned.1.call-done = bf16[768,288]{0,1:T(8,128)(2,1)} async-done(((bf16[768,2304]{0,1:T(8,128)(2,1)}), bf16[768,288]{0,1:T(8,128)(2,1)}) %reduce-scatter.15.cloned.1.call-update) | async-done | bytes 442384 | tf_op jit(solution)/shard_map/reduce_scatter | solution.py:273
  401.8 2.1 copy.101
  404.0 96.3 %reduce-scatter.29.cloned.1.call-done = bf16[384,768]{1,0:T(8,128)(2,1)} async-done(((bf16[3072,768]{1,0:T(8,128)(2,1)}), bf16[384,768]{1,0:T(8,128)(2,1)}) %reduce-scatter.29.cloned.1.call-update) | async-done | bytes 589840
  500.3 2.1 copy.106
  506.3 92.5 %reduce-scatter.21.cloned.1.call-done = bf16[3072,96]{0,1:T(8,128)(2,1)} async-done(((bf16[3072,768]{0,1:T(8,128)(2,1)}), bf16[3072,96]{0,1:T(8,128)(2,1)}) %reduce-scatter.21.cloned.1.call-update) | async-done | bytes 589840 | tf_op jit(solution)/shard_map/reduce_scatter | solution.py:282
  600.5 7.3 fusion.55
  607.8 3.8 slice_reduce_fusion
  611.6 8.4 %add_convert_fusion.1 = bf16[1024,768]{1,0:T(8,128)(2,1)} fusion(f32[1024,768]{1,0:T(8,128)} %copy-done.25, bf16[768,2304]{1,0:T(8,128)(2,1)S(1)} %copy-done, bf16[512,768]{0,1:T(8,128)(2,1)} %bitcast.165, bf16[512,768]{0,1:T(8,128)(2,1)} %bitcast.175, bf16[512,768]{0,1:T(8,128)(2,1)} %bitcast.159, bf16[512,768]{0,1:T(8,128)(2,1)} %bitcast.169, ...), kind=kOutput, calls=%fused_computation.53 | convolution fusion | flops 3653763072 | bytes 12976128 | tf_op jit(solution)/shard_map/re,de->rd/dot_general | solution.py:269
  624.4 21.5 %reduce-scatter.25.cloned.1.call-done = bf16[192,288]{1,0:T(8,128)(2,1)} async-done(((bf16[768,288]{1,0:T(8,128)(2,1)}), bf16[192,288]{1,0:T(8,128)(2,1)}) %reduce-scatter.25.cloned.1.call-update) | async-done | bytes 110608
  649.2 21.3 %reduce-scatter.19.cloned.1.call-done = bf16[192,384]{1,0:T(8,128)(2,1)} async-done(((bf16[768,384]{1,0:T(8,128)(2,1)}), bf16[192,384]{1,0:T(8,128)(2,1)}) %reduce-scatter.19.cloned.1.call-update) | async-done | bytes 147472 | tf_op jit(solution)/shard_map/reduce_scatter | solution.py:293
  672.2 23.2 %reduce-scatter.23.cloned.1.call-done = bf16[768,96]{0,1:T(8,128)(2,1)} async-done(((bf16[3072,96]{0,1:T(8,128)(2,1)}), bf16[768,96]{0,1:T(8,128)(2,1)}) %reduce-scatter.23.cloned.1.call-update) | async-done | bytes 147472 | tf_op jit(solution)/shard_map/reduce_scatter | solution.py:296
  697.0 41.6 %all-reduce.3.cloned.1.call-done = (f32[768]{0:T(1024)}, f32[768]{0:T(1024)}, f32[768]{0:T(1024)}, f32[768]{0:T(1024)}, f32[768]{0:T(1024)}, /*index=5*/f32[3072...) async-done(((f32[768]{0:T(1024)}, f32[768]{0:T(1024)}, f32[768]{0:T(1024)}, f32[768]{0:T(1024)}, f32[768]{0:T(1024)}, ...) | async-done | bytes 86064 | tf_op jit(solution)/shard_map/psum | solution.py:300
  (263 shorter events, 87.2 us)
Async XLA Ops:
  8.0 11.4 %copy-start = (bf16[768,2304]{1,0:T(8,128)(2,1)S(1)}, bf16[768,2304]{1,0:T(8,128)(2,1)}, u32[]{:S(2)}) copy-start(bf16[768,2304]{1,0:T(8,128)(2,1)} %param.24) | copy-start | bytes 10616836
  9.0 5.9 copy-start.47
  9.8 69.3 %copy-start.41 = (f32[768]{0:T(1024)}, f32[768]{0:T(1024)S(1)}, u32[]{:S(2)}) copy-start(f32[768]{0:T(1024)S(1)} %convert_element_type.164) | copy-start | bytes 9220
  16.9 71.4 %copy-start.35 = (f32[1,4,2,128]{3,1,2,0:T(4,128)}, f32[1,4,2,128]{3,1,2,0:T(4,128)S(1)}, u32[]{:S(2)}) copy-start(f32[1,4,2,128]{3,1,2,0:T(4,128)S(1)} %copy.107) | copy-start | bytes 12292
  27.6 13.9 %copy-start.52 = (pred[512]{0:T(512)(128)(4,1)S(1)}, pred[512]{0:T(512)(128)(4,1)}, u32[]{:S(2)}) copy-start(pred[512]{0:T(512)(128)(4,1)} %get-tuple-element.78) | copy-start | bytes 1540
  45.6 4.7 copy-start.31
  45.6 4.7 copy-start.20
  47.5 5.5 copy-start.33
  53.0 10.3 %copy-start.56 = (bf16[12,64,512]{2,1,0:T(8,128)(2,1)}, bf16[12,64,512]{2,1,0:T(8,128)(2,1)S(1)}, u32[]{:S(2)}) copy-start(bf16[12,64,512]{2,1,0:T(8,128)(2,1)S(1)} %fusion.27) | copy-start | bytes 2359300
  56.0 4.5 copy-start.2
  56.1 4.7 copy-start.32
  56.1 4.7 copy-start.18
  57.9 5.3 copy-start.34
  65.0 14.0 %copy-start.6 = (f32[1024,768]{1,0:T(8,128)}, f32[1024,768]{1,0:T(8,128)S(1)}, u32[]{:S(2)}) copy-start(f32[1024,768]{1,0:T(8,128)S(1)} %get-tuple-element.122) | copy-start | bytes 9437188
  65.1 14.0 %copy-start.39 = (f32[1024]{0:T(1024)}, f32[1024]{0:T(1024)S(1)}, u32[]{:S(2)}) copy-start(f32[1024]{0:T(1024)S(1)} %broadcast_multiply_fusion.5) | copy-start | bytes 12292
  65.1 14.0 %slice-start.9 = ((s8[4718592]{0:T(1024)(128)(4,1)}), s8[4194304]{0:T(1024)(128)(4,1)S(1)}, s32[]{:S(2)}) async-start(s8[4718592]{0:T(1024)(128)(4,1)} %bitcast.194), calls=%async_computation.27 | async-start | bytes 8388608
  65.6 13.4 %copy-start.43 = (f32[1024]{0:T(1024)}, f32[1024]{0:T(1024)S(1)}, u32[]{:S(2)}) copy-start(f32[1024]{0:T(1024)S(1)} %add_rsqrt_fusion.1) | copy-start | bytes 12292
  65.7 13.5 %copy-start.49 = (f32[768]{0:T(1024)S(1)}, f32[768]{0:T(1024)}, u32[]{:S(2)}) copy-start(f32[768]{0:T(1024)} %convert_element_type.169) | copy-start | bytes 9220
  65.7 13.4 %slice-start.10 = ((s8[4718592]{0:T(1024)(128)(4,1)}), s8[524288]{0:T(1024)(128)(4,1)S(1)}, s32[]{:S(2)}) async-start(s8[4718592]{0:T(1024)(128)(4,1)} %bitcast.194), calls=%async_computation.28 | async-start | bytes 1048576
  79.0 5.5 copy-start.61
  86.9 43.6 %copy-start.37 = (f32[1024]{0:T(1024)}, f32[1024]{0:T(1024)S(1)}, u32[]{:S(2)}) copy-start(f32[1024]{0:T(1024)S(1)} %add_rsqrt_fusion) | copy-start | bytes 12292
  98.0 26.0 %collective-permute-start.6 = (bf16[32,768]{1,0:T(8,128)(2,1)S(1)}, bf16[32,768]{1,0:T(8,128)(2,1)S(1)}, u32[]{:S(2)}, u32[]{:S(2)}) collective-permute-start(bf16[32,768]{1,0:T(8,128)(2,1)S(1)} %get-tuple-element.105), channel_id=1, source_target_pairs={{0,28},{4,24},{8,20},{12,16},{16,12},{20,8},{24,4},{28,0},{1,29},{... | collective-permute-start | bytes 147464 | tf_op jit(solution)/shard_map/ppermute | solution.py:146
  104.0 19.4 %collective-permute-start.5 = (bf16[32,768]{1,0:T(8,128)(2,1)S(1)}, bf16[32,768]{1,0:T(8,128)(2,1)S(1)}, u32[]{:S(2)}, u32[]{:S(2)}) collective-permute-start(bf16[32,768]{1,0:T(8,128)(2,1)S(1)} %get-tuple-element.106), channel_id=1, source_target_pairs={{0,24},{4,28},{8,16},{12,20},{16,8},{20,12},{24,0},{28,4},{1,25},{... | collective-permute-start | bytes 147464 | tf_op jit(solution)/shard_map/ppermute | solution.py:146
  104.2 18.6 %collective-permute-start.4 = (bf16[32,768]{1,0:T(8,128)(2,1)S(1)}, bf16[32,768]{1,0:T(8,128)(2,1)S(1)}, u32[]{:S(2)}, u32[]{:S(2)}) collective-permute-start(bf16[32,768]{1,0:T(8,128)(2,1)S(1)} %get-tuple-element.107), channel_id=1, source_target_pairs={{0,20},{4,16},{8,28},{12,24},{16,4},{20,0},{24,12},{28,8},{1,21},{... | collective-permute-start | bytes 147464 | tf_op jit(solution)/shard_map/ppermute | solution.py:146
  105.0 17.2 %collective-permute-start.3 = (bf16[32,768]{1,0:T(8,128)(2,1)S(1)}, bf16[32,768]{1,0:T(8,128)(2,1)S(1)}, u32[]{:S(2)}, u32[]{:S(2)}) collective-permute-start(bf16[32,768]{1,0:T(8,128)(2,1)S(1)} %get-tuple-element.108), channel_id=1, source_target_pairs={{0,16},{4,20},{8,24},{12,28},{16,0},{20,4},{24,8},{28,12},{1,17},{... | collective-permute-start | bytes 147464 | tf_op jit(solution)/shard_map/ppermute | solution.py:146
  106.9 5.4 collective-permute-start
  112.4 4.2 collective-permute-start.1
  116.6 5.0 collective-permute-start.2
  152.6 14.3 %all-to-all-start = ((bf16[8,32,768]{2,1,0:T(8,128)(2,1)}), bf16[8,32,768]{2,1,0:T(8,128)(2,1)}, u32[]{:S(2)}, u32[]{:S(2)}) async-start(bf16[8,32,768]{2,1,0:T(8,128)(2,1)} %bitcast.177), calls=%async_computation | async-start | bytes 786432 | tf_op jit(solution)/shard_map/all_to_all | solution.py:182
  157.6 173.4 %reduce-scatter.17.cloned.1.call-start = ((), (), s32[]{:S(2)}) async-start(), calls=%async_computation.10 | async-start | bytes 1327104 | tf_op jit(solution)/shard_map/reduce_scatter | solution.py:276
  175.1 5.1 copy-start.4
  175.1 5.1 copy-start.5
  175.1 5.1 copy-start.36
  175.1 5.1 copy-start.38
  175.1 7.0 slice-start.11
  180.2 15.4 %slice-start.13 = ((s8[4718592]{0:T(1024)(128)(4,1)}), s8[4194304]{0:T(1024)(128)(4,1)S(1)}, s32[]{:S(2)}) async-start(s8[4718592]{0:T(1024)(128)(4,1)} %bitcast.198), calls=%async_computation.31 | async-start | bytes 8388608
  182.1 13.5 %copy-start.22 = (f32[1024,768]{1,0:T(8,128)}, f32[1024,768]{1,0:T(8,128)S(1)}, u32[]{:S(2)}) copy-start(f32[1024,768]{1,0:T(8,128)S(1)} %get-tuple-element.94) | copy-start | bytes 9437188
  182.1 13.5 %copy-start.7 = (f32[1024,768]{1,0:T(8,128)S(1)}, f32[1024,768]{1,0:T(8,128)}, u32[]{:S(2)}) copy-start(f32[1024,768]{1,0:T(8,128)} %copy-done.6) | copy-start | bytes 9437188
  182.1 13.5 %copy-start.40 = (f32[1024]{0:T(1024)S(1)}, f32[1024]{0:T(1024)}, u32[]{:S(2)}) copy-start(f32[1024]{0:T(1024)} %copy-done.39) | copy-start | bytes 12292
  182.1 13.5 %copy-start.42 = (f32[768]{0:T(1024)S(1)}, f32[768]{0:T(1024)}, u32[]{:S(2)}) copy-start(f32[768]{0:T(1024)} %copy-done.41) | copy-start | bytes 9220
  182.2 13.5 %copy-start.44 = (f32[1024]{0:T(1024)S(1)}, f32[1024]{0:T(1024)}, u32[]{:S(2)}) copy-start(f32[1024]{0:T(1024)} %copy-done.43) | copy-start | bytes 12292
  182.2 13.5 %slice-start.14 = ((s8[4718592]{0:T(1024)(128)(4,1)}), s8[524288]{0:T(1024)(128)(4,1)S(1)}, s32[]{:S(2)}) async-start(s8[4718592]{0:T(1024)(128)(4,1)} %bitcast.198), calls=%async_computation.32 | async-start | bytes 1048576
  195.6 6.6 copy-start.60
  212.1 10.7 %copy-start.11 = (bf16[512,768]{0,1:T(8,128)(2,1)}, bf16[512,768]{0,1:T(8,128)(2,1)S(1)}, u32[]{:S(2)}) copy-start(bf16[512,768]{0,1:T(8,128)(2,1)S(1)} %get-tuple-element.103) | copy-start | bytes 2359300
  212.1 10.7 %slice-start = ((s8[12582912]{0:T(1024)(128)(4,1)}), s8[4194304]{0:T(1024)(128)(4,1)S(1)}, s32[]{:S(2)}) async-start(s8[12582912]{0:T(1024)(128)(4,1)} %bitcast.133), calls=%async_computation.18 | async-start | bytes 8388608
  212.1 11.7 %slice-start.1 = ((s8[12582912]{0:T(1024)(128)(4,1)}), s8[4194304]{0:T(1024)(128)(4,1)S(1)}, s32[]{:S(2)}) async-start(s8[12582912]{0:T(1024)(128)(4,1)} %bitcast.133), calls=%async_computation.19 | async-start | bytes 8388608
  212.1 12.9 %slice-start.2 = ((s8[12582912]{0:T(1024)(128)(4,1)}), s8[4194304]{0:T(1024)(128)(4,1)S(1)}, s32[]{:S(2)}) async-start(s8[12582912]{0:T(1024)(128)(4,1)} %bitcast.133), calls=%async_computation.20 | async-start | bytes 8388608
  225.0 10.8 %copy-start.15 = (bf16[512,768]{0,1:T(8,128)(2,1)S(1)}, bf16[512,768]{0,1:T(8,128)(2,1)}, u32[]{:S(2)}) copy-start(bf16[512,768]{0,1:T(8,128)(2,1)} %copy.78) | copy-start | bytes 2359300
  225.0 21.5 %slice-start.6 = ((s8[12582912]{0:T(1024)(128)(4,1)}), s8[4194304]{0:T(1024)(128)(4,1)S(1)}, s32[]{:S(2)}) async-start(s8[12582912]{0:T(1024)(128)(4,1)} %bitcast.137), calls=%async_computation.24 | async-start | bytes 8388608
  225.0 21.5 %slice-start.7 = ((s8[12582912]{0:T(1024)(128)(4,1)}), s8[4194304]{0:T(1024)(128)(4,1)S(1)}, s32[]{:S(2)}) async-start(s8[12582912]{0:T(1024)(128)(4,1)} %bitcast.137), calls=%async_computation.25 | async-start | bytes 8388608
  235.8 5.9 copy-start.10
  235.8 10.7 %slice-start.8 = ((s8[12582912]{0:T(1024)(128)(4,1)}), s8[4194304]{0:T(1024)(128)(4,1)S(1)}, s32[]{:S(2)}) async-start(s8[12582912]{0:T(1024)(128)(4,1)} %bitcast.137), calls=%async_computation.26 | async-start | bytes 8388608
  241.6 4.8 copy-start.30
  256.1 145.7 %reduce-scatter.15.cloned.1.call-start = ((), (), s32[]{:S(2)}) async-start(), calls=%async_computation.9 | async-start | bytes 3981312 | tf_op jit(solution)/shard_map/reduce_scatter | solution.py:273
  256.2 10.8 %copy-start.14 = (bf16[512,768]{0,1:T(8,128)(2,1)S(1)}, bf16[512,768]{0,1:T(8,128)(2,1)}, u32[]{:S(2)}) copy-start(bf16[512,768]{0,1:T(8,128)(2,1)} %copy.82) | copy-start | bytes 2359300
  256.2 14.0 %slice-start.3 = ((s8[12582912]{0:T(1024)(128)(4,1)}), s8[4194304]{0:T(1024)(128)(4,1)S(1)}, s32[]{:S(2)}) async-start(s8[12582912]{0:T(1024)(128)(4,1)} %bitcast.135), calls=%async_computation.21 | async-start | bytes 8388608
  256.2 14.0 %slice-start.4 = ((s8[12582912]{0:T(1024)(128)(4,1)}), s8[4194304]{0:T(1024)(128)(4,1)S(1)}, s32[]{:S(2)}) async-start(s8[12582912]{0:T(1024)(128)(4,1)} %bitcast.135), calls=%async_computation.22 | async-start | bytes 8388608
  303.3 197.0 %reduce-scatter.29.cloned.1.call-start = ((), (), s32[]{:S(2)}) async-start(), calls=%async_computation.16 | async-start | bytes 5308416
  320.7 278.1 %reduce-scatter.21.cloned.1.call-start = ((), (), s32[]{:S(2)}) async-start(), calls=%async_computation.12 | async-start | bytes 5308416 | tf_op jit(solution)/shard_map/reduce_scatter | solution.py:282
  330.9 290.4 %reduce-scatter.27.cloned.1.call-start = ((), (), s32[]{:S(2)}) async-start(), calls=%async_computation.15 | async-start | bytes 245760
  332.7 313.1 %reduce-scatter.25.cloned.1.call-start = ((), (), s32[]{:S(2)}) async-start(), calls=%async_computation.14 | async-start | bytes 737280
  403.9 266.6 %reduce-scatter.19.cloned.1.call-start = ((), (), s32[]{:S(2)}) async-start(), calls=%async_computation.11 | async-start | bytes 737280 | tf_op jit(solution)/shard_map/reduce_scatter | solution.py:293
  502.5 192.9 %reduce-scatter.23.cloned.1.call-start = ((), (), s32[]{:S(2)}) async-start(), calls=%async_computation.13 | async-start | bytes 737280 | tf_op jit(solution)/shard_map/reduce_scatter | solution.py:296
  598.8 139.8 %all-reduce.3.cloned.1.call-start = ((), (), s32[]{:S(2)}) async-start(), calls=%async_computation.17 | async-start | bytes 189440 | tf_op jit(solution)/shard_map/psum | solution.py:300
  (30 other events, 78.2 us)
Sparse Core Ops, SparseCore 0:
  256.3 63.7 reduce-scatter.16
  323.7 78.1 reduce-scatter.14
  405.5 94.8 reduce-scatter.28
  503.8 94.9 reduce-scatter.20
  601.7 19.5 reduce-scatter.26
  623.7 22.1 reduce-scatter.24
  648.5 22.0 reduce-scatter.18
  673.2 22.0 reduce-scatter.22
Sparse Core Ops, SparseCore 1:
  611.7 126.8 all-reduce.2
